TPU v7x, 256 devices: a whole 4x4x8 slice. The times are simulated.
256 devices in a mesh: sp: 64 (over y, z, core), dp: 4 (over x).
Axes of the slice: x: 4, y: 4, z: 8, core: 2. Of those that a mesh axis runs over, the one named last changes fastest.
Arguments:
- volume: bfloat16 [4, 96, 256, 8, 128], P('dp', None, 'sp'), may hold values from -6 to 6
- cotangent: bfloat16 [4, 96, 256, 8, 128], P('dp', None, 'sp'), may hold values from -6 to 6
- kernels_xy: bfloat16 [2, 96, 3, 3], replicated, may hold values from -2 to 2
- kernels_z: bfloat16 [2, 96, 3], replicated, may hold values from -3.5 to 3.5
- mixing: bfloat16 [2, 96, 96], replicated, may hold values from -0.625 to 0.625
Outputs:
- volume_grad: bfloat16 [4, 96, 256, 8, 128], P('dp', None, 'sp')
- mixing_grad: float32 [2, 96, 96], replicated
- xy_grad: float32 [2, 96, 3, 3], replicated
- z_grad: float32 [2, 96, 3], replicated
All inputs are finite; a program needn't handle non-finite values.
Results may differ from a plain program's by a relative error of at most 0.018.
Values may be sent and summed in bfloat16 or wider, within the bound.
A program may use at most 64 MiB of HBM per device.

v0:
```python
import math
import jax
import jax.numpy as jnp
from jax import lax
from jax.sharding import PartitionSpec as P


def padded_2(x, sides, width):
    for axis, dim in sides:
        count, length = (lax.axis_size(axis), x.shape[dim])
        up = [(i, (i + 1) % count) for i in range(count - 1)]
        down = [(j, i) for i, j in up]
        last = lax.slice_in_dim(x, length - width, length, axis=dim)
        first = lax.slice_in_dim(x, 0, width, axis=dim)
        before = lax.ppermute(last, axis, up)
        after = lax.ppermute(first, axis, down)
        x = jnp.concatenate([before, x, after], axis=dim)
    return x


def conv_plane(inputs, kernel):
    extent = inputs.shape[1] - 2
    across = inputs.shape[3]
    padded = jnp.pad(inputs, ((0, 0), (0, 0), (0, 0), (1, 1)))
    summed = jnp.zeros((inputs.shape[0], extent, inputs.shape[2], across), jnp.float32)
    for row_tap in range(3):
        for col_tap in range(3):
            summed = summed + kernel[:, row_tap, col_tap][:, None, None, None] * padded[
                :, row_tap : row_tap + extent, :, col_tap : col_tap + across
            ].astype(jnp.float32)
    return summed


def conv_depth(inputs, kernel):
    depth_len = inputs.shape[2]
    padded = jnp.pad(inputs, ((0, 0), (0, 0), (1, 1), (0, 0)))
    summed = jnp.zeros(inputs.shape, jnp.float32)
    for depth_tap in range(3):
        summed = (
            summed
            + kernel[:, depth_tap][:, None, None, None]
            * padded[:, :, depth_tap : depth_tap + depth_len, :]
        )
    return summed


def mix_channels(weights, inputs):
    channels = inputs.shape[0]
    flat = inputs.reshape(channels, -1)
    return jnp.dot(weights, flat, preferred_element_type=jnp.float32).reshape(inputs.shape)


def forward_block(inputs, kernel_xy, kernel_z, weights):
    planar = conv_plane(inputs, kernel_xy)
    axial = conv_depth(planar, kernel_z).astype(jnp.bfloat16)
    preact = mix_channels(weights, axial)
    return (planar, axial, preact)


def silu_slope(preact):
    sigma = jax.nn.sigmoid(preact)
    return sigma * (1.0 + preact * (1.0 - sigma))


def backward_block(grad_out, planar, axial, preact, around, kernel_z, weights, trim):
    grad_pre = (grad_out.astype(jnp.float32) * silu_slope(preact)).astype(jnp.bfloat16)
    channels = grad_pre.shape[0]
    grad_axial = jnp.dot(
        weights.T, grad_pre.reshape(channels, -1), preferred_element_type=jnp.float32
    ).reshape(grad_pre.shape)
    grad_planar = conv_depth(grad_axial, kernel_z[:, ::-1]).astype(jnp.bfloat16)
    extent = grad_pre.shape[1]
    own_extent = extent - 2 * trim
    own_pre = grad_pre.reshape(channels, -1)
    own_axial = axial.reshape(channels, -1)
    grad_weights = lax.dot_general(
        own_pre, own_axial, (((1,), (1,)), ((), ())), preferred_element_type=jnp.float32
    )
    depth_len = planar.shape[2]
    planar_pad = jnp.pad(planar, ((0, 0), (0, 0), (1, 1), (0, 0)))
    grad_kz = jnp.stack(
        [
            jnp.sum(
                grad_axial * planar_pad[:, :, depth_tap : depth_tap + depth_len, :], axis=(1, 2, 3)
            )
            for depth_tap in range(3)
        ],
        axis=1,
    )
    own_grad_planar = grad_planar.astype(jnp.float32)
    across = around.shape[3]
    around_pad = jnp.pad(around, ((0, 0), (0, 0), (0, 0), (1, 1)))
    rows_list = []
    for row_tap in range(3):
        cols_list = []
        for col_tap in range(3):
            cols_list.append(
                jnp.sum(
                    own_grad_planar
                    * around_pad[
                        :, row_tap : row_tap + own_extent, :, col_tap : col_tap + across
                    ].astype(jnp.float32),
                    axis=(1, 2, 3),
                )
            )
        rows_list.append(jnp.stack(cols_list, axis=1))
    grad_kxy = jnp.stack(rows_list, axis=1)
    return (grad_planar, (grad_weights, grad_kxy, grad_kz))


def edge_grads(grad_planar):
    return padded_2(grad_planar, (("sp", 1),), 1)


def settle_all(lower, upper):
    summed = lax.psum((lower[0], lower[1], lower[2], upper[0], upper[1], upper[2]), ("sp", "dp"))
    return ((summed[0], summed[1], summed[2]), (summed[3], summed[4], summed[5]))


def on_device(volume, cotangent, kernels_xy, kernels_z, mixing):
    inputs = volume[0]
    grad_top = cotangent[0]
    kernel_xy = kernels_xy.astype(jnp.float32)
    kernel_z = kernels_z.astype(jnp.float32)
    slab_len = inputs.shape[1]
    ranks = lax.axis_size("sp")
    place = lax.axis_index("sp")
    wide = padded_2(inputs, (("sp", 1),), 2)
    planar1, axial1, preact1 = forward_block(wide, kernel_xy[0], kernel_z[0], mixing[0])
    hidden = jax.nn.silu(preact1).astype(jnp.bfloat16)
    spots = place * slab_len - 1 + jnp.arange(slab_len + 2, dtype=jnp.int32)
    hidden = jnp.where(
        ((spots >= 0) & (spots < slab_len * ranks))[None, :, None, None],
        hidden,
        jnp.zeros_like(hidden),
    )
    planar2, axial2, preact2 = forward_block(hidden, kernel_xy[1], kernel_z[1], mixing[1])
    grad_planar2, upper = backward_block(
        grad_top, planar2, axial2, preact2, hidden, kernel_z[1], mixing[1], 0
    )
    grad_hidden = conv_plane(edge_grads(grad_planar2), kernel_xy[1][:, ::-1, ::-1]).astype(
        jnp.bfloat16
    )
    grad_planar1, lower = backward_block(
        grad_hidden,
        planar1[:, 1:-1],
        axial1[:, 1:-1],
        preact1[:, 1:-1],
        wide[:, 1:-1],
        kernel_z[0],
        mixing[0],
        0,
    )
    grad_inputs = conv_plane(edge_grads(grad_planar1), kernel_xy[0][:, ::-1, ::-1]).astype(
        jnp.bfloat16
    )
    lower, upper = settle_all(lower, upper)
    factor = 1.0 / math.sqrt(
        lax.axis_size("dp") * slab_len * ranks * inputs.shape[2] * inputs.shape[3]
    )
    mixing_grad = jnp.stack([lower[0], upper[0]]) * factor
    xy_grad = jnp.stack([lower[1], upper[1]]) * factor
    z_grad = jnp.stack([lower[2], upper[2]]) * factor
    return (grad_inputs[None], mixing_grad, xy_grad, z_grad)


def solution(mesh):
    return jax.shard_map(
        on_device,
        mesh=mesh,
        in_specs=(P("dp", None, "sp", None, None), P("dp", None, "sp", None, None), P(), P(), P()),
        out_specs=(P("dp", None, "sp", None, None), P(), P(), P()),
        check_vma=False,
    )
```

profile of v0, /device:TPU:1, one launch (start us, length us, event | category | flops | bytes accessed | tf_op | source)
XLA Modules:
  0.0 328.5 jit_solution(12075035630448840751)
XLA Ops:
  7.2 1.5 copy.76
  8.8 4.9 %collective-permute-start = (bf16[96,2,8,128]{3,0,2,1:T(8,128)(2,1)S(1)}, bf16[96,2,8,128]{3,0,2,1:T(8,128)(2,1)S(1)}, u32[]{:S(2)}, u32[]{:S(2)}) collective-permute-start(bf16[96,2,8,128]{3,0,2,1:T(8,128)(2,1)S(1)} %get-tuple-element.61), channel_id=1, source_target_pairs={{0,4},{4,8},{8,12},{12,16},{16,20},{20,24},{24,28},{28,32},{32,36}... | collective-permute-start | bytes 1179656 | tf_op jit(solution)/shard_map/ppermute | solution.py:15
  13.8 1.9 collective-permute-start.1
  15.8 1.5 reshape.101
  17.3 1.2 collective-permute-done
  18.5 4.4 %collective-permute-done.1 = bf16[96,2,8,128]{3,0,2,1:T(8,128)(2,1)S(1)} collective-permute-done((bf16[96,2,8,128]{3,0,2,1:T(8,128)(2,1)S(1)}, bf16[96,2,8,128]{3,0,2,1:T(8,128)(2,1)S(1)}, u32[]{:S(2)}, u32[]{:S(2)}) %collective-permute-start.1) | collective-permute-done | bytes 393248 | tf_op jit(solution)/shard_map/ppermute | solution.py:16
  23.0 3.1 multiply_add_fusion
  26.1 1.4 copy-done
  27.5 0.5 fusion.15
  28.1 0.5 copy.22
  28.5 0.3 copy-done.6
  28.9 0.5 convolution_bitcast_fusion
  29.3 0.4 copy.41
  29.7 0.6 fusion.79
  30.4 3.0 fusion.24
  33.4 0.6 add_convert_fusion
  34.0 0.4 fusion.84
  34.4 1.0 copy-done.5
  35.4 0.8 convolution_bitcast_fusion.2
  36.5 6.6 %multiply_reduce_fusion.2 = (f32[96]{0:T(128)S(1)}, f32[96]{0:T(128)S(1)}, f32[96]{0:T(128)S(1)}, f32[96]{0:T(128)S(1)}, f32[96]{0:T(128)S(1)}, /*index=5*/f32[9...) fusion(f32[96,4,8,128]{3,2,1,0:T(8,128)S(1)} %bitcast.196, ...), kind=kLoop, calls=%fused_computation.147 | loop fusion | flops 15727488 | bytes 7477248 | tf_op jit(solution)/shard_map/reduce_sum | solution.py:83
  43.1 1.9 collective-permute-start.2
  45.1 2.6 collective-permute-start.3
  47.9 0.6 fusion.69
  48.6 0.6 maximum_bitcast_fusion.9
  49.2 0.6 maximum_bitcast_fusion.1
  49.8 1.2 convolution_bitcast_fusion.3
  51.0 1.4 collective-permute-done.3
  52.3 1.5 fusion.9
  53.9 3.5 %multiply_convert_fusion.1 = bf16[96,4,8,128]{3,2,1,0:T(8,128)(2,1)S(1)} fusion(f32[96,6,8,128]{3,2,1,0:T(8,128)S(1)} %bitcast.193, bf16[96,6,8,130]{3,2,1,0:T(8,128)(2,1)S(1)} %fusion.9, f32[96]{0:T(128)S(1)} %get-tuple-element.71, bf16[96,1,8,128]{3,2,1,0:T(8,128)(2,1)S(1)} %collective-permute-done.3, bf16[96,4,8,128]{3,2,1,0:T(8,128)(2,1)S(1)} %get-tuple-element.56, ...), kind=kLoop, calls=%fused_computation.149 | loop fusion | flops 15335424 | bytes 8260992 | tf_op jit(solution)/shard_map/convert_element_type | solution.py:66
  57.4 1.0 convolution_bitcast_fusion.4
  58.5 0.4 convolution_bitcast_fusion.1
  59.2 0.9 copy-done.1
  60.1 0.6 slice-done
  60.7 1.4 fusion.31
  62.1 0.6 maximum_bitcast_fusion.8
  62.7 2.8 fusion.60
  65.5 0.6 maximum_bitcast_fusion
  66.2 2.1 collective-permute-start.4
  68.3 2.3 collective-permute-start.5
  70.6 242.2 %all-reduce.13.cloned.1.call-done = (f32[1,96,96]{2,1,0:T(8,128)}, f32[1,96,96]{2,1,0:T(8,128)}, f32[1,96,3,3]{1,3,2,0:T(4,128)}, f32[1,96,3,3]{1,3,2,0:T(4,128)...) async-done(((f32[1,96,96]{2,1,0:T(8,128)}, f32[1,96,96]{2,1,0:T(8,128)}, f32[1,96,3,3]{1,3,2,0:T(4,128)}, f32[1,96,3,3]{1,3,2,0:T(4,128)}, f32[1,96,3]{1,2,0:T(4,128)}, ...) | async-done | bytes 82960 | tf_op jit(solution)/shard_map/psum | solution.py:116
  312.8 0.7 maximum_multiply_fusion.2
  313.5 0.6 copy.33
  314.1 0.7 maximum_multiply_fusion.1
  314.8 0.6 copy.32
  315.4 1.5 maximum_multiply_fusion
  316.9 1.6 fusion.11
  318.4 2.0 fusion.92
  320.4 1.2 copy.31
  (44 shorter events, 1.3 us)
Async XLA Ops:
  7.2 8.5 %copy-start.7 = (bf16[2,96,3,3]{1,0,3,2:T(2,128)(2,1)S(1)}, bf16[2,96,3,3]{1,0,3,2:T(2,128)(2,1)}, u32[]{:S(2)}) copy-start(bf16[2,96,3,3]{1,0,3,2:T(2,128)(2,1)} %param.7) | copy-start | bytes 10372
  7.2 8.6 %copy-start.8 = (bf16[2,96,3]{1,0,2:T(2,128)(2,1)S(1)}, bf16[2,96,3]{1,0,2:T(2,128)(2,1)}, u32[]{:S(2)}) copy-start(bf16[2,96,3]{1,0,2:T(2,128)(2,1)} %param.8) | copy-start | bytes 3460
  7.2 8.6 %copy-start.4 = (bf16[1,96,4,8,128]{4,3,2,1,0:T(8,128)(2,1)S(1)}, bf16[1,96,4,8,128]{4,3,2,1,0:T(8,128)(2,1)}, u32[]{:S(2)}) copy-start(bf16[1,96,4,8,128]{4,3,2,1,0:T(8,128)(2,1)} %param.6) | copy-start | bytes 2359300
  7.2 305.6 %all-reduce.13.cloned.1.call-start = ((), (), s32[]{:S(2)}) async-start(), calls=%async_computation | async-start | bytes 229376 | tf_op jit(solution)/shard_map/psum | solution.py:116
  8.8 9.6 %collective-permute-start = (bf16[96,2,8,128]{3,0,2,1:T(8,128)(2,1)S(1)}, bf16[96,2,8,128]{3,0,2,1:T(8,128)(2,1)S(1)}, u32[]{:S(2)}, u32[]{:S(2)}) collective-permute-start(bf16[96,2,8,128]{3,0,2,1:T(8,128)(2,1)S(1)} %get-tuple-element.61), channel_id=1, source_target_pairs={{0,4},{4,8},{8,12},{12,16},{16,20},{20,24},{24,28},{28,32},{32,36}... | collective-permute-start | bytes 1179656 | tf_op jit(solution)/shard_map/ppermute | solution.py:15
  13.8 9.1 %collective-permute-start.1 = (bf16[96,2,8,128]{3,0,2,1:T(8,128)(2,1)S(1)}, bf16[96,2,8,128]{3,0,2,1:T(8,128)(2,1)S(1)}, u32[]{:S(2)}, u32[]{:S(2)}) collective-permute-start(bf16[96,2,8,128]{3,0,2,1:T(8,128)(2,1)S(1)} %get-tuple-element.62), channel_id=1, source_target_pairs={{4,0},{8,4},{12,8},{16,12},{20,16},{24,20},{28,24},{32,28},{36,32}... | collective-permute-start | bytes 1179656 | tf_op jit(solution)/shard_map/ppermute | solution.py:16
  23.0 3.1 copy-start.2
  26.1 1.4 copy-start
  28.1 0.8 copy-start.6
  34.0 1.4 copy-start.5
  43.1 7.8 %collective-permute-start.2 = (bf16[96,1,8,128]{3,2,1,0:T(8,128)(2,1)S(1)}, bf16[96,1,8,128]{3,2,1,0:T(8,128)(2,1)S(1)}, u32[]{:S(2)}, u32[]{:S(2)}) collective-permute-start(bf16[96,1,8,128]{3,2,1,0:T(8,128)(2,1)S(1)} %get-tuple-element.59), channel_id=1, source_target_pairs={{0,4},{4,8},{8,12},{12,16},{16,20},{20,24},{24,28},{28,32},{32,36}... | collective-permute-start | bytes 589832 | tf_op jit(solution)/shard_map/ppermute | solution.py:15
  45.1 7.3 %collective-permute-start.3 = (bf16[96,1,8,128]{3,2,1,0:T(8,128)(2,1)S(1)}, bf16[96,1,8,128]{3,2,1,0:T(8,128)(2,1)S(1)}, u32[]{:S(2)}, u32[]{:S(2)}) collective-permute-start(bf16[96,1,8,128]{3,2,1,0:T(8,128)(2,1)S(1)} %get-tuple-element.60), channel_id=1, source_target_pairs={{4,0},{8,4},{12,8},{16,12},{20,16},{24,20},{28,24},{32,28},{36,32}... | collective-permute-start | bytes 589832 | tf_op jit(solution)/shard_map/ppermute | solution.py:16
  58.5 1.7 copy-start.1
  58.9 1.8 slice-start
  60.7 2.0 slice-start.1
  60.7 2.0 copy-start.3
  66.2 250.6 %collective-permute-start.4 = (bf16[96,1,8,128]{3,0,2,1:T(8,128)(2,1)S(1)}, bf16[96,1,8,128]{3,0,2,1:T(8,128)(2,1)S(1)}, u32[]{:S(2)}, u32[]{:S(2)}) collective-permute-start(bf16[96,1,8,128]{3,0,2,1:T(8,128)(2,1)S(1)} %get-tuple-element.57), channel_id=1, source_target_pairs={{0,4},{4,8},{8,12},{12,16},{16,20},{20,24},{24,28},{28,32},{32,36}... | collective-permute-start | bytes 589832 | tf_op jit(solution)/shard_map/ppermute | solution.py:15
  68.3 248.6 %collective-permute-start.5 = (bf16[96,1,8,128]{3,0,2,1:T(8,128)(2,1)S(1)}, bf16[96,1,8,128]{3,0,2,1:T(8,128)(2,1)S(1)}, u32[]{:S(2)}, u32[]{:S(2)}) collective-permute-start(bf16[96,1,8,128]{3,0,2,1:T(8,128)(2,1)S(1)} %get-tuple-element.58), channel_id=1, source_target_pairs={{4,0},{8,4},{12,8},{16,12},{20,16},{24,20},{28,24},{32,28},{36,32}... | collective-permute-start | bytes 589832 | tf_op jit(solution)/shard_map/ppermute | solution.py:16
Sparse Core Ops, SparseCore 0:
  66.3 246.4 all-reduce.12
where the time goes:
time: 329 us; the launch traced here: 328 us
  waiting for transfers between devices  249 us (76%)
  other arithmetic  33.4 us (10%)
  starting transfers between devices  15.7 us (5%)
  between operations  14.4 us (4%)
  local copies, waits for them, and re-layouts  11.5 us (3%)
  matrix products  4.28 us (1%)
    psum x1, waiting for transfers between devices, settle_all(): lax.psum((lower[0], lower[1], lower[2], upper[0], upper[1], upper[2]), ('...  242 us
    ppermute x3, starting transfers between devices, padded_2(): before = lax.ppermute(last, axis, up)  8.92 us
    unnamed x28, local copies, waits for them, and re-layouts  8.82 us
    reduce_sum x2, other arithmetic, backward_block(): jnp.sum(grad_axial * planar_pad[:, :, depth_tap:depth_tap + depth_len, :]...  7.96 us
    ppermute x3, starting transfers between devices, padded_2(): after = lax.ppermute(first, axis, down)  6.79 us
  transfers between devices with their start and end apart: 7, of which 4 were waited for; matrix products, arithmetic and copies ran while one was open for 3% of the time, Pallas kernels for 0%

commit v1 on v0

--- a/solution.py
+++ b/solution.py
@@ -113,7 +113,9 @@
 
 
 def settle_all(lower, upper):
-    summed = lax.psum((lower[0], lower[1], lower[2], upper[0], upper[1], upper[2]), ("sp", "dp"))
+    summed = lax.psum(
+        lax.psum((lower[0], lower[1], lower[2], upper[0], upper[1], upper[2]), "sp"), "dp"
+    )
     return ((summed[0], summed[1], summed[2]), (summed[3], summed[4], summed[5]))
 
 

time: 329 us -> 304 us (0.924)
  waiting for transfers between devices: 249 us -> 222 us
    psum x1 -> x2, waiting for transfers between devices: 242 us -> 215 us  [the longest x1 176 us: settle_all(): lax.psum((lower[0], lower[1], lower[2], upper[0], upper[1], upper[2]), 'sp')]
  transfers between devices with their start and end apart: 7 -> 8, of which waited for: 4 -> 5; matrix products, arithmetic and copies ran while one was open for 3% -> 3% of each run, Pallas kernels for 0% -> 0%
where the time goes in v1:
time: 304 us; the launch traced here: 302 us
  waiting for transfers between devices  222 us (73%)
  other arithmetic  33.3 us (11%)
  starting transfers between devices  16.8 us (6%)
  between operations  14.5 us (5%)
  local copies, waits for them, and re-layouts  11.5 us (4%)
  matrix products  4.28 us (1%)
    psum x1, waiting for transfers between devices, settle_all(): lax.psum((lower[0], lower[1], lower[2], upper[0], upper[1], upper[2]), 'sp')  176 us
    psum x1, waiting for transfers between devices, settle_all(): lax.psum(lax.psum((lower[0], lower[1], lower[2], upper[0], upper[1], uppe...  38.6 us
    ppermute x3, starting transfers between devices, padded_2(): before = lax.ppermute(last, axis, up)  10.2 us
    unnamed x28, local copies, waits for them, and re-layouts  8.82 us
    reduce_sum x2, other arithmetic, backward_block(): jnp.sum(grad_axial * planar_pad[:, :, depth_tap:depth_tap + depth_len, :]...  7.96 us
    ppermute x3, starting transfers between devices, padded_2(): after = lax.ppermute(first, axis, down)  6.44 us
  transfers between devices with their start and end apart: 8, of which 5 were waited for; matrix products, arithmetic and copies ran while one was open for 3% of the time, Pallas kernels for 0%

profile of v1, /device:TPU:1, one launch (start us, length us, event | category | flops | bytes accessed | tf_op | source)
XLA Modules:
  0.0 302.2 jit_solution(10722703445760988632)
XLA Ops:
  7.2 1.5 copy.76
  8.8 4.9 %collective-permute-start = (bf16[96,2,8,128]{3,0,2,1:T(8,128)(2,1)S(1)}, bf16[96,2,8,128]{3,0,2,1:T(8,128)(2,1)S(1)}, u32[]{:S(2)}, u32[]{:S(2)}) collective-permute-start(bf16[96,2,8,128]{3,0,2,1:T(8,128)(2,1)S(1)} %get-tuple-element.67), channel_id=1, source_target_pairs={{0,4},{4,8},{8,12},{12,16},{16,20},{20,24},{24,28},{28,32},{32,36}... | collective-permute-start | bytes 1179656 | tf_op jit(solution)/shard_map/ppermute | solution.py:15
  13.8 1.9 collective-permute-start.1
  15.8 1.5 reshape.101
  17.3 1.2 collective-permute-done
  18.5 4.4 %collective-permute-done.1 = bf16[96,2,8,128]{3,0,2,1:T(8,128)(2,1)S(1)} collective-permute-done((bf16[96,2,8,128]{3,0,2,1:T(8,128)(2,1)S(1)}, bf16[96,2,8,128]{3,0,2,1:T(8,128)(2,1)S(1)}, u32[]{:S(2)}, u32[]{:S(2)}) %collective-permute-start.1) | collective-permute-done | bytes 393248 | tf_op jit(solution)/shard_map/ppermute | solution.py:16
  23.0 3.1 %multiply_add_fusion = f32[96,6,8,128]{3,0,2,1:T(8,128)S(1)} fusion(bf16[96,2,8,128]{3,0,2,1:T(8,128)(2,1)S(1)} %collective-permute-done.1, bf16[96,4,8,128]{3,0,2,1:T(8,128)(2,1)S(1)} %bitcast.184, bf16[96,2,8,128]{3,0,2,1:T(8,128)(2,1)S(1)} %collective-permute-done, bf16[96,8,8,128]{3,0,2,1:T(8,128)(2,1)S(1)} %pad_maximum_fusion, ...), kind=kLoop, calls=%fused_computation.66 | loop fusion | flops 18874368 | bytes 6689280 | tf_op jit(solution)/shard_map/add | solution.py:28
  26.1 1.4 copy-done
  27.5 0.5 fusion.15
  28.1 0.5 copy.22
  28.9 0.5 convolution_bitcast_fusion
  29.3 0.4 copy.41
  29.7 0.6 fusion.79
  30.4 3.0 %fusion.24 = f32[96,4,8,128]{3,2,1,0:T(8,128)S(1)} fusion(f32[96]{0:T(128)S(1)} %get-tuple-element.70, f32[96]{0:T(128)S(1)} %get-tuple-element.71, f32[96]{0:T(128)S(1)} %get-tuple-element.72, f32[96]{0:T(128)S(1)} %get-tuple-element.73, f32[96]{0:T(128)S(1)} %get-tuple-element.74, f32[96]{0:T(128)S(1)} %get-tuple-element.75, f32[96]{0:T(128)S(1)} %get-tuple-element.76, ...), kind=kLoop, calls=%fused_computation.88 | loop fusion | flops 10223616 | bytes 5116416 | tf_op jit(solution)/shard_map/add | solution.py:28
  33.4 0.6 add_convert_fusion
  34.0 0.4 fusion.84
  34.4 1.0 copy-done.5
  35.4 0.8 convolution_bitcast_fusion.2
  36.5 6.6 %multiply_reduce_fusion.2 = (f32[96]{0:T(128)S(1)}, f32[96]{0:T(128)S(1)}, f32[96]{0:T(128)S(1)}, f32[96]{0:T(128)S(1)}, f32[96]{0:T(128)S(1)}, /*index=5*/f32[9...) fusion(f32[96,4,8,128]{3,2,1,0:T(8,128)S(1)} %bitcast.190, ...), kind=kLoop, calls=%fused_computation.147 | loop fusion | flops 15727488 | bytes 7477248 | tf_op jit(solution)/shard_map/reduce_sum | solution.py:83
  43.1 1.9 collective-permute-start.2
  45.1 2.6 collective-permute-start.3
  47.9 0.6 fusion.69
  48.6 0.6 pad_maximum_fusion.10
  49.2 0.6 pad_maximum_fusion.8
  49.8 1.2 convolution_bitcast_fusion.3
  51.0 1.4 collective-permute-done.3
  52.3 1.5 fusion.9
  53.9 3.5 %multiply_convert_fusion.1 = bf16[96,4,8,128]{3,2,1,0:T(8,128)(2,1)S(1)} fusion(f32[96,6,8,128]{3,2,1,0:T(8,128)S(1)} %bitcast.187, bf16[96,6,8,130]{3,2,1,0:T(8,128)(2,1)S(1)} %fusion.9, f32[96]{0:T(128)S(1)} %get-tuple-element.77, bf16[96,1,8,128]{3,2,1,0:T(8,128)(2,1)S(1)} %collective-permute-done.3, bf16[96,4,8,128]{3,2,1,0:T(8,128)(2,1)S(1)} %get-tuple-element.62, ...), kind=kLoop, calls=%fused_computation.149 | loop fusion | flops 15335424 | bytes 8260992 | tf_op jit(solution)/shard_map/convert_element_type | solution.py:66
  57.4 1.0 convolution_bitcast_fusion.4
  58.5 0.4 convolution_bitcast_fusion.1
  59.2 0.9 copy-done.1
  60.1 0.6 slice-done
  60.7 1.4 fusion.31
  62.1 0.6 pad_maximum_fusion.9
  62.7 2.8 fusion.60
  65.5 0.6 pad_maximum_fusion.7
  66.2 176.3 %all-reduce.15.cloned.1.call-done = (f32[96,96]{1,0:T(8,128)}, f32[96,96]{1,0:T(8,128)}, f32[96,3,3]{0,2,1:T(4,128)}, f32[96,3,3]{0,2,1:T(4,128)}, f32[96,3]{0,1:T(4,128)}, /*index=5*/f32[96,3]{0,1:T(4,128)}) async-done(((f32[96,96]{1,0:T(8,128)}, f32[96,96]{1,0:T(8,128)}, f32[96,3,3]{0,2,1:T(4,128)}, f32[96,3,3]{0,2,1:T(4,128)}, f32[96,3]{0,1:T(4,128)}, /*index=5*/f32[96,3]{0,1:T(4,128)}), ...) | async-done | bytes 82960 | tf_op jit(solution)/shard_map/psum | solution.py:117
  242.5 3.4 %collective-permute-start.4 = (bf16[96,1,8,128]{3,0,2,1:T(8,128)(2,1)S(1)}, bf16[96,1,8,128]{3,0,2,1:T(8,128)(2,1)S(1)}, u32[]{:S(2)}, u32[]{:S(2)}) collective-permute-start(bf16[96,1,8,128]{3,0,2,1:T(8,128)(2,1)S(1)} %get-tuple-element.63), channel_id=1, source_target_pairs={{0,4},{4,8},{8,12},{12,16},{16,20},{20,24},{24,28},{28,32},{32,36}... | collective-permute-start | bytes 589832 | tf_op jit(solution)/shard_map/ppermute | solution.py:15
  245.9 1.9 collective-permute-start.5
  247.9 38.6 %all-reduce.17.cloned.1.call-done = (f32[1,96,96]{2,1,0:T(8,128)}, f32[1,96,96]{2,1,0:T(8,128)}, f32[1,96,3,3]{1,3,2,0:T(4,128)}, f32[1,96,3,3]{1,3,2,0:T(4,128)...) async-done(((f32[1,96,96]{2,1,0:T(8,128)}, f32[1,96,96]{2,1,0:T(8,128)}, f32[1,96,3,3]{1,3,2,0:T(4,128)}, f32[1,96,3,3]{1,3,2,0:T(4,128)}, f32[1,96,3]{1,2,0:T(4,128)}, ...) | async-done | bytes 82960 | tf_op jit(solution)/shard_map/psum | solution.py:116
  286.5 0.7 maximum_multiply_fusion.2
  287.2 0.6 copy.33
  287.7 0.7 maximum_multiply_fusion.1
  288.5 0.6 copy.32
  289.1 1.5 maximum_multiply_fusion
  290.5 1.6 fusion.11
  292.1 2.0 fusion.92
  294.1 1.2 copy.31
  (47 shorter events, 1.7 us)
Async XLA Ops:
  7.2 8.5 %copy-start.7 = (bf16[2,96,3,3]{1,0,3,2:T(2,128)(2,1)S(1)}, bf16[2,96,3,3]{1,0,3,2:T(2,128)(2,1)}, u32[]{:S(2)}) copy-start(bf16[2,96,3,3]{1,0,3,2:T(2,128)(2,1)} %param.7) | copy-start | bytes 10372
  7.2 8.6 %copy-start.8 = (bf16[2,96,3]{1,0,2:T(2,128)(2,1)S(1)}, bf16[2,96,3]{1,0,2:T(2,128)(2,1)}, u32[]{:S(2)}) copy-start(bf16[2,96,3]{1,0,2:T(2,128)(2,1)} %param.8) | copy-start | bytes 3460
  7.2 8.6 %copy-start.4 = (bf16[1,96,4,8,128]{4,3,2,1,0:T(8,128)(2,1)S(1)}, bf16[1,96,4,8,128]{4,3,2,1,0:T(8,128)(2,1)}, u32[]{:S(2)}) copy-start(bf16[1,96,4,8,128]{4,3,2,1,0:T(8,128)(2,1)} %param.6) | copy-start | bytes 2359300
  7.2 235.3 %all-reduce.15.cloned.1.call-start = ((), (), s32[]{:S(2)}) async-start(), calls=%async_computation | async-start | bytes 229376 | tf_op jit(solution)/shard_map/psum | solution.py:117
  8.8 9.6 %collective-permute-start = (bf16[96,2,8,128]{3,0,2,1:T(8,128)(2,1)S(1)}, bf16[96,2,8,128]{3,0,2,1:T(8,128)(2,1)S(1)}, u32[]{:S(2)}, u32[]{:S(2)}) collective-permute-start(bf16[96,2,8,128]{3,0,2,1:T(8,128)(2,1)S(1)} %get-tuple-element.67), channel_id=1, source_target_pairs={{0,4},{4,8},{8,12},{12,16},{16,20},{20,24},{24,28},{28,32},{32,36}... | collective-permute-start | bytes 1179656 | tf_op jit(solution)/shard_map/ppermute | solution.py:15
  13.8 9.1 %collective-permute-start.1 = (bf16[96,2,8,128]{3,0,2,1:T(8,128)(2,1)S(1)}, bf16[96,2,8,128]{3,0,2,1:T(8,128)(2,1)S(1)}, u32[]{:S(2)}, u32[]{:S(2)}) collective-permute-start(bf16[96,2,8,128]{3,0,2,1:T(8,128)(2,1)S(1)} %get-tuple-element.68), channel_id=1, source_target_pairs={{4,0},{8,4},{12,8},{16,12},{20,16},{24,20},{28,24},{32,28},{36,32}... | collective-permute-start | bytes 1179656 | tf_op jit(solution)/shard_map/ppermute | solution.py:16
  23.0 3.1 %copy-start.2 = (bf16[96,8,8,128]{3,0,2,1:T(8,128)(2,1)}, bf16[96,8,8,128]{3,0,2,1:T(8,128)(2,1)S(1)}, u32[]{:S(2)}) copy-start(bf16[96,8,8,128]{3,0,2,1:T(8,128)(2,1)S(1)} %pad_maximum_fusion) | copy-start | bytes 4718596
  26.1 1.4 copy-start
  28.1 0.8 copy-start.6
  34.0 1.4 copy-start.5
  43.1 7.8 %collective-permute-start.2 = (bf16[96,1,8,128]{3,2,1,0:T(8,128)(2,1)S(1)}, bf16[96,1,8,128]{3,2,1,0:T(8,128)(2,1)S(1)}, u32[]{:S(2)}, u32[]{:S(2)}) collective-permute-start(bf16[96,1,8,128]{3,2,1,0:T(8,128)(2,1)S(1)} %get-tuple-element.65), channel_id=1, source_target_pairs={{0,4},{4,8},{8,12},{12,16},{16,20},{20,24},{24,28},{28,32},{32,36}... | collective-permute-start | bytes 589832 | tf_op jit(solution)/shard_map/ppermute | solution.py:15
  45.1 7.3 %collective-permute-start.3 = (bf16[96,1,8,128]{3,2,1,0:T(8,128)(2,1)S(1)}, bf16[96,1,8,128]{3,2,1,0:T(8,128)(2,1)S(1)}, u32[]{:S(2)}, u32[]{:S(2)}) collective-permute-start(bf16[96,1,8,128]{3,2,1,0:T(8,128)(2,1)S(1)} %get-tuple-element.66), channel_id=1, source_target_pairs={{4,0},{8,4},{12,8},{16,12},{20,16},{24,20},{28,24},{32,28},{36,32}... | collective-permute-start | bytes 589832 | tf_op jit(solution)/shard_map/ppermute | solution.py:16
  58.5 1.7 copy-start.1
  58.9 1.8 slice-start
  60.7 2.0 slice-start.1
  60.7 2.0 copy-start.3
  66.1 220.3 %all-reduce.17.cloned.1.call-start = ((), (), s32[]{:S(2)}) async-start(), calls=%async_computation.1 | async-start | bytes 229376 | tf_op jit(solution)/shard_map/psum | solution.py:116
  242.5 48.0 %collective-permute-start.4 = (bf16[96,1,8,128]{3,0,2,1:T(8,128)(2,1)S(1)}, bf16[96,1,8,128]{3,0,2,1:T(8,128)(2,1)S(1)}, u32[]{:S(2)}, u32[]{:S(2)}) collective-permute-start(bf16[96,1,8,128]{3,0,2,1:T(8,128)(2,1)S(1)} %get-tuple-element.63), channel_id=1, source_target_pairs={{0,4},{4,8},{8,12},{12,16},{16,20},{20,24},{24,28},{28,32},{32,36}... | collective-permute-start | bytes 589832 | tf_op jit(solution)/shard_map/ppermute | solution.py:15
  245.9 44.6 %collective-permute-start.5 = (bf16[96,1,8,128]{3,0,2,1:T(8,128)(2,1)S(1)}, bf16[96,1,8,128]{3,0,2,1:T(8,128)(2,1)S(1)}, u32[]{:S(2)}, u32[]{:S(2)}) collective-permute-start(bf16[96,1,8,128]{3,0,2,1:T(8,128)(2,1)S(1)} %get-tuple-element.64), channel_id=1, source_target_pairs={{4,0},{8,4},{12,8},{16,12},{20,16},{24,20},{28,24},{32,28},{36,32}... | collective-permute-start | bytes 589832 | tf_op jit(solution)/shard_map/ppermute | solution.py:16
Sparse Core Ops, SparseCore 0:
  66.3 176.1 all-reduce.14
  245.2 41.2 all-reduce.16
